TPU v7x, 256 devices: a whole 4x4x8 slice. The times are simulated.
256 devices in a mesh: dp: 32 (over x, y, core), mp: 8 (over z).
Axes of the slice: x: 4, y: 4, z: 8, core: 2. Of those that a mesh axis runs over, the one named last changes fastest.
Arguments:
- features: bfloat16 [65536, 2, 512], P('dp'), may hold values from -27 to 27
- projection: bfloat16 [512, 256], replicated, may hold values from -1 to 1
- prototypes: float32 [3000, 256], P('mp'), may hold values from -7 to 7
Outputs:
- grad_prototypes: float32 [3000, 256], P('mp')
- grad_projection: float32 [512, 256], replicated
- loss: float32 [], replicated
All inputs are finite; a program needn't handle non-finite values.
Results may differ from a plain program's by a relative error of at most 0.0019.
The roundings to bfloat16 on the way count: a program that leaves them out, or rounds other values in their place, can miss the bound.
Values may be sent and summed in bfloat16 or wider, within the bound.
A program may use at most 128 MiB of HBM per device.

v0:
```python
import jax
import jax.numpy as jnp
from jax import lax
from jax.sharding import PartitionSpec as P

ITERS = 3
EPSILON_CODES = 0.05
SOFTMAX_TEMPER = 0.1
LOSS_FACTOR = 4096.0
TINY = 1e-06


def unit_rows(values):
    inverse = lax.rsqrt(jnp.sum(values * values, axis=-1, keepdims=True) + TINY)
    return (values * inverse, inverse)


def prototype_totals(values):
    return lax.psum(jnp.sum(values, axis=0), "dp")


def code_totals(values):
    return lax.psum(jnp.sum(values, axis=-1), "mp")


def loss_pieces(
    prototype_logits, softmax_exponent, softmax_denominator, assignments, gradient_factor
):
    swapped_targets = assignments[:, ::-1]
    grad_half = (
        (softmax_exponent / softmax_denominator[..., None] - swapped_targets) * gradient_factor
    ).astype(jnp.bfloat16)
    loss_portion = jnp.sum(
        swapped_targets
        * (prototype_logits * (1.0 / SOFTMAX_TEMPER) - jnp.log(softmax_denominator)[..., None])
    )
    return (grad_half, loss_portion)


def embed_backward(grad_unit, embed_unit, embed_inverse, own_feats):
    along_unit = jnp.sum(embed_unit * grad_unit, axis=-1, keepdims=True)
    grad_raw = ((grad_unit - embed_unit * along_unit) * embed_inverse).astype(jnp.bfloat16)
    return jnp.einsum("bve,bvp->ep", own_feats, grad_raw, preferred_element_type=jnp.float32)


def body(features, projection, prototypes):
    local_rows = features.shape[0]
    own_count = local_rows // lax.axis_size("mp")
    batch_row_count = local_rows * lax.axis_size("dp")
    gradient_factor = LOSS_FACTOR / (2.0 * batch_row_count * SOFTMAX_TEMPER)
    proto_unit, proto_inverse = unit_rows(prototypes)
    proto_half = proto_unit.astype(jnp.bfloat16)
    first_row = lax.axis_index("mp") * own_count
    own_feats = lax.dynamic_slice_in_dim(features, first_row, own_count, 0)
    raw_embed = jnp.einsum("bve,ep->bvp", own_feats, projection, preferred_element_type=jnp.float32)
    embed_unit, embed_inverse = unit_rows(raw_embed)
    embed_half = embed_unit.astype(jnp.bfloat16)
    all_embed = lax.all_gather(embed_half, "mp", axis=0, tiled=True)
    prototype_logits = jnp.einsum(
        "bvp,kp->bvk", all_embed, proto_half, preferred_element_type=jnp.float32
    )
    transport = jnp.exp(prototype_logits * (1.0 / EPSILON_CODES))
    softmax_exponent = jnp.exp(prototype_logits * (1.0 / SOFTMAX_TEMPER))
    soft_part = jnp.sum(softmax_exponent, axis=-1)
    for iteration in range(ITERS - 1):
        transport = transport / prototype_totals(transport)[None]
        transport = transport / code_totals(transport)[..., None]
    transport = transport / prototype_totals(transport)[None]
    softmax_denominator = lax.psum(soft_part, "mp")
    row_sums = code_totals(transport)
    assignments = transport / row_sums[..., None]
    grad_half, loss_portion = loss_pieces(
        prototype_logits, softmax_exponent, softmax_denominator, assignments, gradient_factor
    )
    proto_grad = jnp.einsum("bvk,bvp->kp", grad_half, all_embed, preferred_element_type=jnp.float32)
    proto_grad = lax.psum(proto_grad, "dp")
    grad_unit = lax.psum_scatter(
        jnp.einsum("bvk,kp->bvp", grad_half, proto_half, preferred_element_type=jnp.float32),
        "mp",
        scatter_dimension=0,
        tiled=True,
    )
    weight_part = embed_backward(grad_unit, embed_unit, embed_inverse, own_feats)
    weight_grad, loss_total = lax.psum((weight_part, loss_portion), ("dp", "mp"))
    along_proto = jnp.sum(proto_unit * proto_grad, axis=-1, keepdims=True)
    grad_protos = (proto_grad - proto_unit * along_proto) * proto_inverse
    loss_value = -loss_total / (2.0 * batch_row_count)
    return (grad_protos, weight_grad, loss_value)


def solution(mesh):
    return jax.shard_map(
        body,
        mesh=mesh,
        in_specs=(P("dp", None, None), P(), P("mp", None)),
        out_specs=(P("mp", None), P(), P()),
        check_vma=False,
    )
```

profile of v0, /device:TPU:2, one launch (start us, length us, event | category | flops | bytes accessed | tf_op | source)
XLA Modules:
  0.0 803.6 jit_solution(7048572155357733132)
XLA Ops:
  7.2 1.4 constant_dynamic-slice_fusion
  8.7 0.8 copy-done.3
  9.5 0.4 multiply_reduce_fusion.1
  9.9 0.7 multiply_convert_fusion.1
  10.7 1.1 multiply_reduce_fusion.4
  11.8 49.1 %all-gather.2.cloned.1.call-done = bf16[2048,2,256]{0,2,1:T(8,128)(2,1)} async-done(((bf16[256,2,256]{0,2,1:T(8,128)(2,1)}), bf16[2048,2,256]{0,2,1:T(8,128)(2,1)}) %all-gather.2.cloned.1.call-update) | async-done | bytes 2097168 | tf_op jit(solution)/shard_map/all_gather | solution.py:58
  60.9 5.4 fusion.12
  66.3 53.0 %psum.71 = f32[2,375]{1,0:T(2,128)S(1)} all-reduce(f32[2,375]{1,0:T(2,128)S(1)} %get-tuple-element.11), channel_id=1, replica_groups=mesh['dp'=32,'mp'=8] {'dp'}, use_global_device_ids=true, to_apply=%region_5.0 | all-reduce | flops 750 | bytes 6000 | tf_op jit(solution)/shard_map/psum | solution.py:19
  119.3 3.8 exponential_reduce_fusion
  123.2 29.9 %psum.72 = f32[2048,2]{0,1:T(2,128)S(1)} all-reduce(f32[2048,2]{0,1:T(2,128)S(1)} %get-tuple-element.4), channel_id=1, replica_groups=mesh['dp'=32,'mp'=8] {'mp'}, use_global_device_ids=true, to_apply=%region_7.0 | all-reduce | flops 4096 | bytes 32768 | tf_op jit(solution)/shard_map/psum | solution.py:23
  153.0 4.4 fusion.8
  157.5 54.7 %psum.73 = f32[2,375]{1,0:T(2,128)S(1)} all-reduce(f32[2,375]{1,0:T(2,128)S(1)} %fusion.8), channel_id=1, replica_groups=mesh['dp'=32,'mp'=8] {'dp'}, use_global_device_ids=true, to_apply=%region_9.0 | all-reduce | flops 750 | bytes 6000 | tf_op jit(solution)/shard_map/psum | solution.py:19
  212.1 3.7 fusion.9
  215.9 27.0 %psum.74 = f32[2048,2]{0,1:T(2,128)S(1)} all-reduce(f32[2048,2]{0,1:T(2,128)S(1)} %fusion.9), channel_id=1, replica_groups=mesh['dp'=32,'mp'=8] {'mp'}, use_global_device_ids=true, to_apply=%region_11.0 | all-reduce | flops 4096 | bytes 32768 | tf_op jit(solution)/shard_map/psum | solution.py:23
  242.9 3.9 fusion.10
  246.8 62.7 %psum.75 = f32[2,375]{1,0:T(2,128)S(1)} all-reduce(f32[2,375]{1,0:T(2,128)S(1)} %fusion.10), channel_id=1, replica_groups=mesh['dp'=32,'mp'=8] {'dp'}, use_global_device_ids=true, to_apply=%region_13.0 | all-reduce | flops 750 | bytes 6000 | tf_op jit(solution)/shard_map/psum | solution.py:19
  309.5 4.3 fusion.11
  313.8 27.7 %all-reduce = (f32[2048,2]{0,1:T(2,128)S(1)}, f32[2048,2]{0,1:T(2,128)S(1)}) all-reduce(f32[2048,2]{0,1:T(2,128)S(1)} %fusion.11, f32[2048,2]{0,1:T(2,128)S(1)} %get-tuple-element.3), channel_id=1, replica_groups=mesh['dp'=32,'mp'=8] {'mp'}, use_global_device_ids=true, to_apply=%region_15.0 | all-reduce | flops 8192 | bytes 65536 | tf_op jit(solution)/shard_map/psum | solution.py:23
  341.5 5.1 fusion.7
  346.7 2.6 multiply_reduce_fusion
  349.2 1.6 copy-done.1
  350.9 3.3 fusion.28
  354.2 0.0 all-reduce.4.cloned.1.call-start
  354.3 4.3 convolution_bitcast_fusion.1
  358.7 0.0 all-reduce.6.cloned.1.call-start
  358.7 90.6 %psum.79 = f32[]{:T(128)} all-reduce(f32[]{:T(128)} %get-tuple-element.7), channel_id=1, replica_groups=mesh['dp'=32,'mp'=8] {'dp','mp'}, use_global_device_ids=true, to_apply=%region_22.0 | all-reduce | flops 1 | bytes 8 | tf_op jit(solution)/shard_map/psum | solution.py:84
  450.0 2.5 convolution_bitcast_fusion
  452.5 83.7 %all-reduce.4.cloned.1.call-done = f32[375,256]{1,0:T(8,128)} async-done(((f32[375,256]{1,0:T(8,128)}), f32[375,256]{1,0:T(8,128)}) %all-reduce.4.cloned.1.call-update) | async-done | bytes 384016 | tf_op jit(solution)/shard_map/psum | solution.py:76
  536.2 1.2 multiply_reduce_fusion.3
  537.4 1.9 subtract_multiply_fusion
  539.3 254.8 %all-reduce.6.cloned.1.call-done = f32[512,256]{1,0:T(8,128)} async-done(((f32[512,256]{1,0:T(8,128)}), f32[512,256]{1,0:T(8,128)}) %all-reduce.6.cloned.1.call-update) | async-done | bytes 524304 | tf_op jit(solution)/shard_map/psum | solution.py:84
  794.1 1.9 copy.29
  (23 shorter events, 0.2 us)
Async XLA Ops:
  7.2 2.3 copy-start
  7.2 53.7 %all-gather.2.cloned.1.call-start = ((), (), s32[]{:S(2)}) async-start(), calls=%async_computation.1 | async-start | bytes 2359296 | tf_op jit(solution)/shard_map/all_gather | solution.py:58
  8.7 0.8 copy-start.3
  10.6 439.3 %reduce-scatter.2.cloned.1.call-start = ((), (), s32[]{:S(2)}) async-start(), calls=%async_computation.3 | async-start | bytes 4718592 | tf_op jit(solution)/shard_map/reduce_scatter | solution.py:77
  309.5 37.1 %slice-start = ((s8[6160384]{0:T(1024)(128)(4,1)}), s8[1966080]{0:T(1024)(128)(4,1)S(1)}, s32[]{:S(2)}) async-start(s8[6160384]{0:T(1024)(128)(4,1)} %bitcast.19), calls=%async_computation.5 | async-start | bytes 3932160
  341.5 5.1 slice-start.1
  346.7 4.2 copy-start.2
  349.2 1.6 copy-start.1
  354.2 95.8 %copy-start.4 = (bf16[256,2,512]{2,1,0:T(2,128)(2,1)S(1)}, bf16[256,2,512]{2,1,0:T(2,128)(2,1)}, u32[]{:S(2)}) copy-start(bf16[256,2,512]{2,1,0:T(2,128)(2,1)} %copy-done.3) | copy-start | bytes 1572868
  354.2 181.9 %all-reduce.4.cloned.1.call-start = ((), (), s32[]{:S(2)}) async-start(), calls=%async_computation.2 | async-start | bytes 770048 | tf_op jit(solution)/shard_map/psum | solution.py:76
  358.7 435.4 %all-reduce.6.cloned.1.call-start = ((), (), s32[]{:S(2)}) async-start(), calls=%async_computation.4 | async-start | bytes 1048576 | tf_op jit(solution)/shard_map/psum | solution.py:84
Sparse Core Ops, SparseCore 0:
  10.7 50.1 all-gather.1
  354.4 66.9 reduce-scatter.1
  425.2 110.8 all-reduce.3
  542.1 251.9 all-reduce.5
where the time goes:
time: 804 us
  waiting for transfers between devices  388 us (48%)
  blocking collectives  345 us (43%)
  other arithmetic  32.9 us (4%)
  matrix products  16 us (2%)
  between operations  15.7 us (2%)
    psum x1, waiting for transfers between devices, body(): lax.psum((weight_part, loss_portion), ('dp', 'mp'))  255 us
    psum x3, blocking collectives, prototype_totals(): return lax.psum(jnp.sum(values, axis=0), 'dp')  170 us
    psum x1, blocking collectives, body(): lax.psum((weight_part, loss_portion), ('dp', 'mp'))  90.6 us
    psum x3, blocking collectives, code_totals(): return lax.psum(jnp.sum(values, axis=-1), 'mp')  84.6 us
    psum x1, waiting for transfers between devices, body(): proto_grad = lax.psum(proto_grad, 'dp')  83.7 us
    all_gather x1, waiting for transfers between devices, body(): all_embed = lax.all_gather(embed_half, 'mp', axis=0, tiled=True)  49.1 us
  transfers between devices with their start and end apart: 4, of which 3 were waited for; matrix products, arithmetic and copies ran while one was open for 1% of the time, Pallas kernels for 0%

commit v1 on v0

--- a/solution.py
+++ b/solution.py
@@ -8,6 +8,11 @@
 SOFTMAX_TEMPER = 0.1
 LOSS_FACTOR = 4096.0
 TINY = 1e-06
+
+
+def all_by_exchange(array, mesh_axis, dim):
+    repeated = jnp.stack([array] * lax.axis_size(mesh_axis))
+    return jnp.concatenate(lax.all_to_all(repeated, mesh_axis, 0, 0), axis=dim)
 
 
 def unit_rows(values):
@@ -55,7 +60,7 @@
     raw_embed = jnp.einsum("bve,ep->bvp", own_feats, projection, preferred_element_type=jnp.float32)
     embed_unit, embed_inverse = unit_rows(raw_embed)
     embed_half = embed_unit.astype(jnp.bfloat16)
-    all_embed = lax.all_gather(embed_half, "mp", axis=0, tiled=True)
+    all_embed = all_by_exchange(embed_half, "mp", 0)
     prototype_logits = jnp.einsum(
         "bvp,kp->bvk", all_embed, proto_half, preferred_element_type=jnp.float32
     )

time: 804 us -> 763 us (0.949)
  waiting for transfers between devices: 388 us -> 335 us
  starting transfers between devices: 0.16 us -> 8.59 us
    psum x1, waiting for transfers between devices: 83.7 us -> 29.8 us  [body(): proto_grad = lax.psum(proto_grad, 'dp')]
    all_to_all x0 -> x1, waiting for transfers between devices: none -> 51 us  [all_by_exchange(): return jnp.concatenate(lax.all_to_all(repeated, mesh_axis, 0, 0), axis=dim)]
    all_gather x1 -> x0, waiting for transfers between devices: 49.1 us -> none  [body(): all_embed = lax.all_gather(embed_half, 'mp', axis=0, tiled=True)]
    all_to_all x0 -> x1, starting transfers between devices: none -> 8.46 us  [all_by_exchange(): return jnp.concatenate(lax.all_to_all(repeated, mesh_axis, 0, 0), axis=dim)]
where the time goes in v1:
time: 763 us; the launch traced here: 762 us
  blocking collectives  347 us (45%)
  waiting for transfers between devices  335 us (44%)
  other arithmetic  31.5 us (4%)
  between operations  17.4 us (2%)
  matrix products  13.7 us (2%)
  local copies, waits for them, and re-layouts  9 us (1%)
  starting transfers between devices  8.59 us (1%)
    psum x1, waiting for transfers between devices, body(): lax.psum((weight_part, loss_portion), ('dp', 'mp'))  254 us
    psum x3, blocking collectives, prototype_totals(): return lax.psum(jnp.sum(values, axis=0), 'dp')  173 us
    psum x1, blocking collectives, body(): lax.psum((weight_part, loss_portion), ('dp', 'mp'))  91.2 us
    psum x3, blocking collectives, code_totals(): return lax.psum(jnp.sum(values, axis=-1), 'mp')  83.4 us
    all_to_all x1, waiting for transfers between devices, all_by_exchange(): return jnp.concatenate(lax.all_to_all(repeated, mesh_axis, 0, 0), axis=dim)  51 us
    psum x1, waiting for transfers between devices, body(): proto_grad = lax.psum(proto_grad, 'dp')  29.8 us
  transfers between devices with their start and end apart: 4, of which 3 were waited for; matrix products, arithmetic and copies ran while one was open for 1% of the time, Pallas kernels for 0%

profile of v1, /device:TPU:2, one launch (start us, length us, event | category | flops | bytes accessed | tf_op | source)
XLA Modules:
  0.0 762.3 jit_solution(14065735646661791606)
XLA Ops:
  8.0 1.5 constant_dynamic-slice_fusion
  9.5 0.8 copy-done.5
  10.3 0.4 multiply_reduce_fusion.1
  10.9 1.6 stack.2
  12.4 8.5 %all-to-all-start = ((bf16[8,256,2,256]{3,1,2,0:T(8,128)(2,1)}), bf16[8,256,2,256]{3,1,2,0:T(8,128)(2,1)S(1)}, u32[]{:S(2)}, u32[]{:S(2)}) async-start(bf16[8,256,2,256]{3,1,2,0:T(8,128)(2,1)} %stack.2), calls=%async_computation | async-start | bytes 4194304 | tf_op jit(solution)/shard_map/all_to_all | solution.py:15
  20.9 0.1 multiply_reduce_fusion.4
  21.1 51.0 %all-to-all-done = bf16[8,256,2,256]{3,1,2,0:T(8,128)(2,1)S(1)} async-done(((bf16[8,256,2,256]{3,1,2,0:T(8,128)(2,1)}), bf16[8,256,2,256]{3,1,2,0:T(8,128)(2,1)S(1)}, u32[]{:S(2)}, u32[]{:S(2)}) %all-to-all-start) | async-done | bytes 2097184 | tf_op jit(solution)/shard_map/all_to_all | solution.py:15
  72.2 1.4 copy-done.3
  73.6 3.7 fusion.12
  77.3 53.0 %psum.71 = f32[2,375]{1,0:T(2,128)S(1)} all-reduce(f32[2,375]{1,0:T(2,128)S(1)} %get-tuple-element.11), channel_id=1, replica_groups=mesh['dp'=32,'mp'=8] {'dp'}, use_global_device_ids=true, to_apply=%region_5.0 | all-reduce | flops 750 | bytes 6000 | tf_op jit(solution)/shard_map/psum | solution.py:24
  130.3 3.8 exponential_reduce_fusion
  134.1 28.7 %psum.72 = f32[2048,2]{0,1:T(2,128)S(1)} all-reduce(f32[2048,2]{0,1:T(2,128)S(1)} %get-tuple-element.4), channel_id=1, replica_groups=mesh['dp'=32,'mp'=8] {'mp'}, use_global_device_ids=true, to_apply=%region_7.0 | all-reduce | flops 4096 | bytes 32768 | tf_op jit(solution)/shard_map/psum | solution.py:28
  162.8 4.5 fusion.8
  167.3 56.9 %psum.73 = f32[2,375]{1,0:T(2,128)S(1)} all-reduce(f32[2,375]{1,0:T(2,128)S(1)} %fusion.8), channel_id=1, replica_groups=mesh['dp'=32,'mp'=8] {'dp'}, use_global_device_ids=true, to_apply=%region_9.0 | all-reduce | flops 750 | bytes 6000 | tf_op jit(solution)/shard_map/psum | solution.py:24
  224.2 3.8 fusion.9
  227.9 27.0 %psum.74 = f32[2048,2]{0,1:T(2,128)S(1)} all-reduce(f32[2048,2]{0,1:T(2,128)S(1)} %fusion.9), channel_id=1, replica_groups=mesh['dp'=32,'mp'=8] {'mp'}, use_global_device_ids=true, to_apply=%region_11.0 | all-reduce | flops 4096 | bytes 32768 | tf_op jit(solution)/shard_map/psum | solution.py:28
  255.0 3.9 fusion.10
  258.9 62.7 %psum.75 = f32[2,375]{1,0:T(2,128)S(1)} all-reduce(f32[2,375]{1,0:T(2,128)S(1)} %fusion.10), channel_id=1, replica_groups=mesh['dp'=32,'mp'=8] {'dp'}, use_global_device_ids=true, to_apply=%region_13.0 | all-reduce | flops 750 | bytes 6000 | tf_op jit(solution)/shard_map/psum | solution.py:24
  321.6 4.4 fusion.11
  326.0 27.7 %all-reduce = (f32[2048,2]{0,1:T(2,128)S(1)}, f32[2048,2]{0,1:T(2,128)S(1)}) all-reduce(f32[2048,2]{0,1:T(2,128)S(1)} %fusion.11, f32[2048,2]{0,1:T(2,128)S(1)} %get-tuple-element.3), channel_id=1, replica_groups=mesh['dp'=32,'mp'=8] {'mp'}, use_global_device_ids=true, to_apply=%region_15.0 | all-reduce | flops 8192 | bytes 65536 | tf_op jit(solution)/shard_map/psum | solution.py:28
  353.7 5.1 fusion.7
  358.8 2.6 multiply_reduce_fusion
  361.5 1.6 copy-done.1
  363.1 3.3 fusion.28
  366.5 3.7 convolution_bitcast_fusion.1
  370.3 91.2 %psum.79 = f32[]{:T(128)} all-reduce(f32[]{:T(128)} %get-tuple-element.7), channel_id=1, replica_groups=mesh['dp'=32,'mp'=8] {'dp','mp'}, use_global_device_ids=true, to_apply=%region_22.0 | all-reduce | flops 1 | bytes 8 | tf_op jit(solution)/shard_map/psum | solution.py:89
  462.1 2.6 convolution_bitcast_fusion
  464.8 29.8 %all-reduce.4.cloned.1.call-done = f32[375,256]{1,0:T(8,128)} async-done(((f32[375,256]{1,0:T(8,128)}), f32[375,256]{1,0:T(8,128)}) %all-reduce.4.cloned.1.call-update) | async-done | bytes 384016 | tf_op jit(solution)/shard_map/psum | solution.py:81
  494.7 1.2 multiply_reduce_fusion.3
  495.9 1.9 subtract_multiply_fusion
  497.8 254.1 %all-reduce.6.cloned.1.call-done = f32[512,256]{1,0:T(8,128)} async-done(((f32[512,256]{1,0:T(8,128)}), f32[512,256]{1,0:T(8,128)}) %all-reduce.6.cloned.1.call-update) | async-done | bytes 524304 | tf_op jit(solution)/shard_map/psum | solution.py:89
  751.9 1.9 copy.33
  (27 shorter events, 0.6 us)
Async XLA Ops:
  8.0 2.3 copy-start
  8.0 12.9 %copy-start.2 = (f32[375,256]{1,0:T(8,128)S(1)}, f32[375,256]{1,0:T(8,128)}, u32[]{:S(2)}) copy-start(f32[375,256]{1,0:T(8,128)} %param.5) | copy-start | bytes 1152004
  9.5 0.8 copy-start.5
  12.4 59.7 %all-to-all-start = ((bf16[8,256,2,256]{3,1,2,0:T(8,128)(2,1)}), bf16[8,256,2,256]{3,1,2,0:T(8,128)(2,1)S(1)}, u32[]{:S(2)}, u32[]{:S(2)}) async-start(bf16[8,256,2,256]{3,1,2,0:T(8,128)(2,1)} %stack.2), calls=%async_computation | async-start | bytes 4194304 | tf_op jit(solution)/shard_map/all_to_all | solution.py:15
  20.9 441.3 %reduce-scatter.2.cloned.1.call-start = ((), (), s32[]{:S(2)}) async-start(), calls=%async_computation.3 | async-start | bytes 4718592 | tf_op jit(solution)/shard_map/reduce_scatter | solution.py:82
  72.2 1.4 copy-start.3
  321.6 37.2 %slice-start = ((s8[6160384]{0:T(1024)(128)(4,1)}), s8[1966080]{0:T(1024)(128)(4,1)S(1)}, s32[]{:S(2)}) async-start(s8[6160384]{0:T(1024)(128)(4,1)} %bitcast.20), calls=%async_computation.5 | async-start | bytes 3932160
  353.7 5.2 slice-start.1
  361.5 1.6 copy-start.1
  361.5 5.1 copy-start.4
  366.5 128.2 %all-reduce.4.cloned.1.call-start = ((), (), s32[]{:S(2)}) async-start(), calls=%async_computation.2 | async-start | bytes 770048 | tf_op jit(solution)/shard_map/psum | solution.py:81
  370.2 381.7 %all-reduce.6.cloned.1.call-start = ((), (), s32[]{:S(2)}) async-start(), calls=%async_computation.4 | async-start | bytes 1048576 | tf_op jit(solution)/shard_map/psum | solution.py:89
Sparse Core Ops, SparseCore 0:
  366.6 66.9 reduce-scatter.1
Sparse Core Ops, SparseCore 1:
  370.8 123.8 all-reduce.3
  500.0 251.8 all-reduce.5
